TPU v7x, 128 devices: a whole 4x4x4 slice. The times are simulated.
128 devices in a mesh: grp: 8 (over z, core), dir: 16 (over x, y).
Axes of the slice: x: 4, y: 4, z: 4, core: 2. Of those that a mesh axis runs over, the one named last changes fastest.
Arguments:
- incident: float32 [4, 1024, 256, 128], P(None, ('grp', 'dir')), may hold values from -6 to 6
- currents_past: bfloat16 [2, 1024, 256, 128], P(None, ('grp', 'dir')), may hold values from -6 to 6
- spectra_past: bfloat16 [2, 128, 1152, 128], P(None, ('grp', 'dir')), may hold values from -9 to 9
- self_inverse: bfloat16 [1024, 256, 256], P(('grp', 'dir')), may hold values from -0.25 to 0.25
- near_blocks: bfloat16 [1024, 6, 2, 256, 256], P(('grp', 'dir')), may hold values from -0.078125 to 0.078125
- neighbours: int32 [1024, 6], P(('grp', 'dir')), may hold values from 0 to 1023, as said below
- near_mask: int32 [1024, 6], P(('grp', 'dir')), may hold values 0 or 1
- ray_out: bfloat16 [256, 1152], replicated, may hold values from -0.375 to 0.375
- ray_in: bfloat16 [1152, 256], replicated, may hold values from -0.1875 to 0.1875
- child_shift: float32 [8, 1152], replicated, may hold values from -1 to 1
- far_sources: int32 [128, 16], replicated, may hold values from 0 to 127
- far_delays: int32 [128, 16], replicated, may hold values from 1 to 2
- translation: float32 [128, 16, 1152], P(None, None, ('grp', 'dir')), may hold values from -0.75 to 0.75
Outputs:
- currents: bfloat16 [4, 1024, 256, 128], P(None, ('grp', 'dir'))
Inputs may be any that keep to these rules, and one draw needn't show every extreme that they name: `neighbours`: the entry of group g names a group held by the same device as g, by the device just before it or by the one just after it, devices counted in the order grp then dir, each holding 8 consecutive groups.
All inputs are finite; a program needn't handle non-finite values. No bound on the sum of `near_mask` on one device may be relied on, other than what follows from the above.
Results may differ from a plain program's by a relative error of at most 0.0095.
Values may be sent and summed in bfloat16 or wider, within the bound.
No kernel may reach another device: no remote copies, remote signals or barrier semaphores. Data moves between devices by JAX's collectives and lax.ppermute only.
A program may use at most 128 MiB of HBM per device.

v0:
```python
import jax
import jax.numpy as jnp
from jax import lax
from jax.sharding import PartitionSpec as P

LAGS = 2
STEPS = 4


def shifted(block, axis, distance):
    devices = range(lax.axis_size(axis))
    route = [(i - distance, i) for i in devices if i - distance in devices]
    return lax.ppermute(block, axis, route)


def window(stacked):
    beside = [shifted(stacked, ("grp", "dir"), offset) for offset in (1, -1)]
    return jnp.concatenate([beside[0], stacked, beside[1]], axis=1)


def to_bands(spectra):
    return lax.all_to_all(spectra, ("grp", "dir"), split_axis=1, concat_axis=0, tiled=True)


def from_bands(incoming):
    return lax.all_to_all(incoming, ("grp", "dir"), split_axis=0, concat_axis=1, tiled=True)


def far_table(far_sources, far_delays, translation, lag_count):
    parents = far_sources.shape[0]
    slot_index = (far_delays - 1) * parents + far_sources
    columns_ids = jnp.arange(lag_count * parents, dtype=jnp.int32)
    onehot = (slot_index[:, :, None] == columns_ids[None, None, :]).astype(jnp.float32)
    return jnp.einsum("ofs,ofk->osk", onehot, translation, precision=lax.Precision.HIGHEST)


def translate(bands, far_weights):
    stacked = jnp.stack(bands).astype(jnp.float32)
    merged = stacked.reshape(
        stacked.shape[0] * stacked.shape[1], stacked.shape[2], stacked.shape[3]
    )
    return jnp.einsum("osk,skr->okr", far_weights, merged, precision=lax.Precision.HIGHEST).astype(
        jnp.bfloat16
    )


def on_device(
    incident,
    currents_past,
    spectra_past,
    self_inverse,
    near_blocks,
    neighbours,
    near_mask,
    ray_out,
    ray_in,
    child_shift,
    far_sources,
    far_delays,
    translation,
):
    groups = self_inverse.shape[0]
    unknowns = self_inverse.shape[1]
    columns = incident.shape[3]
    children = child_shift.shape[0]
    parents = groups // children
    first_group = (lax.axis_index(("grp", "dir")) - 1) * groups
    local_ids = neighbours - first_group
    live_slots = near_mask.astype(jnp.bfloat16)[:, :, None, None, None]
    far_weights = far_table(far_sources, far_delays, translation, LAGS)
    opening = window(currents_past)
    windows = [opening[lag_index] for lag_index in range(LAGS)]
    bands = [to_bands(spectra_past[lag_index]) for lag_index in range(LAGS)]
    results = []
    for step_index in range(STEPS):
        picked = jnp.stack([windows[lag_index][local_ids] for lag_index in range(LAGS)], axis=2)
        near = jnp.einsum(
            "gnlef,gnlfr->ger", near_blocks, picked * live_slots, preferred_element_type=jnp.float32
        )
        incoming = translate(bands, far_weights)
        arriving = from_bands(incoming)
        received = (child_shift[None, :, :, None] * arriving[:, None]).astype(jnp.bfloat16)
        far_part = jnp.einsum("ke,pckr->pcer", ray_in, received, preferred_element_type=jnp.float32)
        far_part = far_part.reshape(groups, unknowns, columns)
        drive = (incident[step_index] - near - far_part).astype(jnp.bfloat16)
        current = jnp.einsum(
            "gef,gfr->ger", self_inverse, drive, preferred_element_type=jnp.float32
        ).astype(jnp.bfloat16)
        results.append(current)
        if step_index + 1 < STEPS:
            spread = jnp.einsum(
                "ek,pcer->pckr",
                ray_out,
                current.reshape(parents, children, unknowns, columns),
                preferred_element_type=jnp.float32,
            )
            spectra = jnp.sum(child_shift[None, :, :, None] * spread, axis=1).astype(jnp.bfloat16)
            bands = [to_bands(spectra)] + bands[:-1]
            windows = [window(current[None])[0]] + windows[:-1]
    return jnp.stack(results)


def solution(mesh):
    in_specs = (
        P(None, ("grp", "dir"), None, None),
        P(None, ("grp", "dir"), None, None),
        P(None, ("grp", "dir"), None, None),
        P(("grp", "dir"), None, None),
        P(("grp", "dir"), None, None, None, None),
        P(("grp", "dir"), None),
        P(("grp", "dir"), None),
        P(),
        P(),
        P(),
        P(),
        P(),
        P(None, None, ("grp", "dir")),
    )
    out_specs = P(None, ("grp", "dir"), None, None)
    return jax.shard_map(
        on_device, mesh=mesh, in_specs=in_specs, out_specs=out_specs, check_vma=False
    )
```

profile of v0, /device:TPU:1, one launch (start us, length us, event | category | flops | bytes accessed | tf_op | source)
XLA Modules:
  0.0 383.6 jit_solution(4717984606406887576)
XLA Ops:
  4.2 6.1 %collective-permute-start.1 = (bf16[2,8,256,128]{3,2,1,0:T(8,128)(2,1)}, bf16[2,8,256,128]{3,2,1,0:T(8,128)(2,1)}, u32[]{:S(2)}, u32[]{:S(2)}) collective-permute-start(bf16[2,8,256,128]{3,2,1,0:T(8,128)(2,1)} %param.14), channel_id=1, source_target_pairs={{1,0},{2,1},{3,2},{4,3},{5,4},{6,5},{7,6},{8,7},{9,8},{10,9},{11,1... | collective-permute-start | bytes 3145736 | tf_op jit(solution)/shard_map/ppermute | solution.py:13
  16.6 6.7 %reduce.16 = bf16[1152,128]{1,0:T(8,128)(2,1)S(1)} reduce(bf16[1152,1,128]{2,1,0:T(2,128)(2,1)S(1)} %bitcast.224, bf16[]{:T(256)} %broadcast.67), dimensions={1}, to_apply=%bitcast.211.reduce_sub_computation | reduce | bytes 589826
  24.3 7.5 %all-to-all-start.1 = ((bf16[128,2,576]{2,1,0:T(2,128)(2,1)}), bf16[128,2,576]{2,1,0:T(2,128)(2,1)S(1)}, u32[]{:S(2)}, u32[]{:S(2)}) async-start(bf16[128,2,576]{2,1,0:T(2,128)(2,1)} %reshape.240), calls=%async_computation.1 | async-start | bytes 655360 | tf_op jit(solution)/shard_map/all_to_all | solution.py:22
  37.1 6.7 %reduce.17 = bf16[1152,128]{1,0:T(8,128)(2,1)S(1)} reduce(bf16[1152,1,128]{2,1,0:T(2,128)(2,1)S(1)} %bitcast.226, bf16[]{:T(256)} %broadcast.67), dimensions={1}, to_apply=%bitcast.212.reduce_sub_computation | reduce | bytes 589826
  47.3 10.6 %all-to-all-start = ((bf16[128,2,576]{2,1,0:T(2,128)(2,1)}), bf16[128,2,576]{2,1,0:T(2,128)(2,1)}, u32[]{:S(2)}, u32[]{:S(2)}) async-start(bf16[128,2,576]{2,1,0:T(2,128)(2,1)} %reshape.242), calls=%async_computation | async-start | bytes 655360 | tf_op jit(solution)/shard_map/all_to_all | solution.py:22
  80.8 9.2 %all-to-all-start.2 = ((bf16[128,9,128]{2,1,0:T(8,128)(2,1)}), bf16[128,9,128]{2,1,0:T(8,128)(2,1)}, u32[]{:S(2)}, u32[]{:S(2)}) async-start(bf16[128,9,128]{2,1,0:T(8,128)(2,1)} %copy.100), calls=%async_computation.2 | async-start | bytes 1048576 | tf_op jit(solution)/shard_map/all_to_all | solution.py:26
  96.8 6.0 %all-to-all-done.2 = bf16[128,9,128]{2,1,0:T(8,128)(2,1)} async-done(((bf16[128,9,128]{2,1,0:T(8,128)(2,1)}), bf16[128,9,128]{2,1,0:T(8,128)(2,1)}, u32[]{:S(2)}, u32[]{:S(2)}) %all-to-all-start.2) | async-done | bytes 294944 | tf_op jit(solution)/shard_map/all_to_all | solution.py:26
  128.8 11.9 %fusion.47 = f32[8,256,128]{1,2,0:T(8,128)} fusion(bf16[8,6,2,256,256]{4,3,2,1,0:T(8,128)(2,1)} %param.17, bf16[8,6,1,256,128]{3,4,1,0,2:T(8,128)(2,1)} %copy.92, bf16[8,6,1,256,128]{3,4,1,0,2:T(8,128)(2,1)} %copy.91, bf16[8,6]{1,0:T(8,128)(2,1)S(1)} %convert_element_type.187, f32[1,8,256,128]{2,3,1,0:T(8,128)} %copy.138), kind=kOutput, calls=%fused_computation.68 | convolution fusion | flops 1617166336 | bytes 20971616 | tf_op jit(solution)/shard_map/gnlef,gnlfr->ger/dot_general | solution.py:77
  148.8 7.5 %reduce.18 = bf16[1152,128]{1,0:T(8,128)(2,1)} reduce(bf16[1152,1,128]{2,1,0:T(2,128)(2,1)S(1)} %bitcast.227, bf16[]{:T(256)} %broadcast.67), dimensions={1}, to_apply=%bitcast.189.reduce_sub_computation | reduce | bytes 589826
  158.2 5.7 %all-to-all-start.3 = ((bf16[128,2,576]{2,1,0:T(2,128)(2,1)}), bf16[128,2,576]{2,1,0:T(2,128)(2,1)}, u32[]{:S(2)}, u32[]{:S(2)}) async-start(bf16[128,2,576]{2,1,0:T(2,128)(2,1)} %reshape.244), calls=%async_computation.3 | async-start | bytes 655360 | tf_op jit(solution)/shard_map/all_to_all | solution.py:22
  166.4 7.3 %collective-permute-start.3 = (bf16[1,8,256,128]{2,3,1,0:T(8,128)(2,1)}, bf16[1,8,256,128]{2,3,1,0:T(8,128)(2,1)}, u32[]{:S(2)}, u32[]{:S(2)}) collective-permute-start(bf16[1,8,256,128]{2,3,1,0:T(8,128)(2,1)} %bitcast.17), channel_id=1, source_target_pairs={{1,0},{2,1},{3,2},{4,3},{5,4},{6,5},{7,6},{8,7},{9,8},{10,9},{11,1... | collective-permute-start | bytes 1572872 | tf_op jit(solution)/shard_map/ppermute | solution.py:13
  187.2 9.9 %all-to-all-start.4 = ((bf16[128,9,128]{2,1,0:T(8,128)(2,1)}), bf16[128,9,128]{2,1,0:T(8,128)(2,1)S(1)}, u32[]{:S(2)}, u32[]{:S(2)}) async-start(bf16[128,9,128]{2,1,0:T(8,128)(2,1)} %copy.108), calls=%async_computation.4 | async-start | bytes 1048576 | tf_op jit(solution)/shard_map/all_to_all | solution.py:26
  203.7 11.8 %fusion.53 = f32[8,256,128]{1,2,0:T(8,128)} fusion(bf16[8,6,2,256,256]{4,3,2,1,0:T(8,128)(2,1)} %param.17, bf16[8,6,1,256,128]{3,4,1,0,2:T(8,128)(2,1)} %copy.91, bf16[8,6,1,256,128]{3,4,1,0,2:T(8,128)(2,1)} %bitcast.217, bf16[8,6]{1,0:T(8,128)(2,1)S(1)} %convert_element_type.187, f32[1,8,256,128]{2,3,1,0:T(8,128)} %copy.139), kind=kOutput, calls=%fused_computation.70 | convolution fusion | flops 1617166336 | bytes 20971616 | tf_op jit(solution)/shard_map/gnlef,gnlfr->ger/dot_general | solution.py:77
  225.8 7.7 %reduce.19 = bf16[1152,128]{1,0:T(8,128)(2,1)S(1)} reduce(bf16[1152,1,128]{2,1,0:T(2,128)(2,1)} %bitcast.228, bf16[]{:T(256)} %broadcast.67), dimensions={1}, to_apply=%bitcast.191.reduce_sub_computation | reduce | bytes 589826
  234.5 9.8 %all-to-all-start.5 = ((bf16[128,2,576]{2,1,0:T(2,128)(2,1)}), bf16[128,2,576]{2,1,0:T(2,128)(2,1)S(1)}, u32[]{:S(2)}, u32[]{:S(2)}) async-start(bf16[128,2,576]{2,1,0:T(2,128)(2,1)} %reshape.246), calls=%async_computation.5 | async-start | bytes 655360 | tf_op jit(solution)/shard_map/all_to_all | solution.py:22
  246.9 7.0 %collective-permute-start.5 = (bf16[1,8,256,128]{2,3,1,0:T(8,128)(2,1)}, bf16[1,8,256,128]{2,3,1,0:T(8,128)(2,1)}, u32[]{:S(2)}, u32[]{:S(2)}) collective-permute-start(bf16[1,8,256,128]{2,3,1,0:T(8,128)(2,1)} %bitcast.35), channel_id=1, source_target_pairs={{1,0},{2,1},{3,2},{4,3},{5,4},{6,5},{7,6},{8,7},{9,8},{10,9},{11,1... | collective-permute-start | bytes 1572872 | tf_op jit(solution)/shard_map/ppermute | solution.py:13
  257.4 6.6 %bitcast_reduce_fusion.1 = bf16[1152,128]{1,0:T(8,128)(2,1)} fusion(bf16[1152,1,128]{2,1,0:T(2,128)(2,1)} %reshape.247), kind=kLoop, calls=%fused_computation.128 | loop fusion | bytes 589824 | tf_op jit(solution)/shard_map/all_to_all | solution.py:22
  267.4 10.3 %all-to-all-start.6 = ((bf16[128,9,128]{2,1,0:T(8,128)(2,1)}), bf16[128,9,128]{2,1,0:T(8,128)(2,1)}, u32[]{:S(2)}, u32[]{:S(2)}) async-start(bf16[128,9,128]{2,1,0:T(8,128)(2,1)} %copy.115), calls=%async_computation.6 | async-start | bytes 1048576 | tf_op jit(solution)/shard_map/all_to_all | solution.py:26
  284.4 11.8 %fusion.59 = f32[8,256,128]{1,2,0:T(8,128)} fusion(bf16[8,6,2,256,256]{4,3,2,1,0:T(8,128)(2,1)} %param.17, bf16[8,6,1,256,128]{3,4,1,0,2:T(8,128)(2,1)} %bitcast.218, bf16[8,6,1,256,128]{3,4,1,0,2:T(8,128)(2,1)} %bitcast.215, bf16[8,6]{1,0:T(8,128)(2,1)S(1)} %convert_element_type.187, f32[1,8,256,128]{2,3,1,0:T(8,128)} %copy.140), kind=kOutput, calls=%fused_computation.72 | convolution fusion | flops 1617166336 | bytes 20971616 | tf_op jit(solution)/shard_map/gnlef,gnlfr->ger/dot_general | solution.py:77
  306.6 7.5 %reduce.20 = bf16[1152,128]{1,0:T(8,128)(2,1)} reduce(bf16[1152,1,128]{2,1,0:T(2,128)(2,1)S(1)} %bitcast.225, bf16[]{:T(256)} %broadcast.67), dimensions={1}, to_apply=%bitcast.193.reduce_sub_computation | reduce | bytes 589826
  316.0 10.2 %all-to-all-start.7 = ((bf16[128,2,576]{2,1,0:T(2,128)(2,1)}), bf16[128,2,576]{2,1,0:T(2,128)(2,1)}, u32[]{:S(2)}, u32[]{:S(2)}) async-start(bf16[128,2,576]{2,1,0:T(2,128)(2,1)} %reshape.248), calls=%async_computation.7 | async-start | bytes 655360 | tf_op jit(solution)/shard_map/all_to_all | solution.py:22
  328.8 7.0 %collective-permute-start.7 = (bf16[1,8,256,128]{2,3,1,0:T(8,128)(2,1)}, bf16[1,8,256,128]{2,3,1,0:T(8,128)(2,1)}, u32[]{:S(2)}, u32[]{:S(2)}) collective-permute-start(bf16[1,8,256,128]{2,3,1,0:T(8,128)(2,1)} %bitcast.52), channel_id=1, source_target_pairs={{1,0},{2,1},{3,2},{4,3},{5,4},{6,5},{7,6},{8,7},{9,8},{10,9},{11,1... | collective-permute-start | bytes 1572872 | tf_op jit(solution)/shard_map/ppermute | solution.py:13
  349.4 9.9 %all-to-all-start.8 = ((bf16[128,9,128]{2,1,0:T(8,128)(2,1)}), bf16[128,9,128]{2,1,0:T(8,128)(2,1)S(1)}, u32[]{:S(2)}, u32[]{:S(2)}) async-start(bf16[128,9,128]{2,1,0:T(8,128)(2,1)} %copy.122), calls=%async_computation.8 | async-start | bytes 1048576 | tf_op jit(solution)/shard_map/all_to_all | solution.py:26
  363.4 11.8 %fusion.65 = f32[8,256,128]{1,2,0:T(8,128)} fusion(bf16[8,6,2,256,256]{4,3,2,1,0:T(8,128)(2,1)} %param.17, bf16[8,6,1,256,128]{3,4,1,0,2:T(8,128)(2,1)} %bitcast.216, bf16[8,6,1,256,128]{3,4,1,0,2:T(8,128)(2,1)} %bitcast.219, bf16[8,6]{1,0:T(8,128)(2,1)S(1)} %convert_element_type.187, f32[1,8,256,128]{2,3,1,0:T(8,128)} %copy.141), kind=kOutput, calls=%fused_computation.74 | convolution fusion | flops 1617166336 | bytes 20971616 | tf_op jit(solution)/shard_map/gnlef,gnlfr->ger/dot_general | solution.py:77
  (121 shorter events, 176.6 us)
Async XLA Ops:
  0.0 140.7 %copy-start = (bf16[8,256,256]{2,1,0:T(8,128)(2,1)S(1)}, bf16[8,256,256]{2,1,0:T(8,128)(2,1)}, u32[]{:S(2)}) copy-start(bf16[8,256,256]{2,1,0:T(8,128)(2,1)} %param.16) | copy-start | bytes 3145732
  0.0 31.8 %copy-start.2 = (f32[128,16,9]{0,1,2:T(8,128)S(1)}, f32[128,16,9]{0,1,2:T(8,128)}, u32[]{:S(2)}) copy-start(f32[128,16,9]{0,1,2:T(8,128)} %param.25) | copy-start | bytes 221188
  0.0 32.3 %copy-start.3 = (s32[128,16]{0,1:T(8,128)S(1)}, s32[128,16]{0,1:T(8,128)}, u32[]{:S(2)}) copy-start(s32[128,16]{0,1:T(8,128)} %param.23) | copy-start | bytes 24580
  0.0 32.3 %copy-start.4 = (s32[128,16]{0,1:T(8,128)S(1)}, s32[128,16]{0,1:T(8,128)}, u32[]{:S(2)}) copy-start(s32[128,16]{0,1:T(8,128)} %param.24) | copy-start | bytes 24580
  0.0 105.0 %collective-permute-start = (bf16[2,8,256,128]{3,2,1,0:T(8,128)(2,1)}, bf16[2,8,256,128]{3,2,1,0:T(8,128)(2,1)}, u32[]{:S(2)}, u32[]{:S(2)}) collective-permute-start(bf16[2,8,256,128]{3,2,1,0:T(8,128)(2,1)} %param.14), channel_id=1, source_target_pairs={{0,1},{1,2},{2,3},{3,4},{4,5},{5,6},{6,7},{7,8},{8,9},{9,10},{10,1... | collective-permute-start | bytes 3145736 | tf_op jit(solution)/shard_map/ppermute | solution.py:13
  4.2 103.5 %collective-permute-start.1 = (bf16[2,8,256,128]{3,2,1,0:T(8,128)(2,1)}, bf16[2,8,256,128]{3,2,1,0:T(8,128)(2,1)}, u32[]{:S(2)}, u32[]{:S(2)}) collective-permute-start(bf16[2,8,256,128]{3,2,1,0:T(8,128)(2,1)} %param.14), channel_id=1, source_target_pairs={{1,0},{2,1},{3,2},{4,3},{5,4},{6,5},{7,6},{8,7},{9,8},{10,9},{11,1... | collective-permute-start | bytes 3145736 | tf_op jit(solution)/shard_map/ppermute | solution.py:13
  24.3 23.0 %all-to-all-start.1 = ((bf16[128,2,576]{2,1,0:T(2,128)(2,1)}), bf16[128,2,576]{2,1,0:T(2,128)(2,1)S(1)}, u32[]{:S(2)}, u32[]{:S(2)}) async-start(bf16[128,2,576]{2,1,0:T(2,128)(2,1)} %reshape.240), calls=%async_computation.1 | async-start | bytes 655360 | tf_op jit(solution)/shard_map/all_to_all | solution.py:22
  32.5 25.4 %copy-start.6 = (s32[8,6]{1,0:T(8,128)S(1)}, s32[8,6]{1,0:T(8,128)}, u32[]{:S(2)}) copy-start(s32[8,6]{1,0:T(8,128)} %param.18) | copy-start | bytes 580
  32.5 25.5 %copy-start.5 = (s32[8,6]{1,0:T(8,128)S(1)}, s32[8,6]{1,0:T(8,128)}, u32[]{:S(2)}) copy-start(s32[8,6]{1,0:T(8,128)} %param.19) | copy-start | bytes 580
  47.3 22.0 %all-to-all-start = ((bf16[128,2,576]{2,1,0:T(2,128)(2,1)}), bf16[128,2,576]{2,1,0:T(2,128)(2,1)}, u32[]{:S(2)}, u32[]{:S(2)}) async-start(bf16[128,2,576]{2,1,0:T(2,128)(2,1)} %reshape.242), calls=%async_computation | async-start | bytes 655360 | tf_op jit(solution)/shard_map/all_to_all | solution.py:22
  80.8 22.0 %all-to-all-start.2 = ((bf16[128,9,128]{2,1,0:T(8,128)(2,1)}), bf16[128,9,128]{2,1,0:T(8,128)(2,1)}, u32[]{:S(2)}, u32[]{:S(2)}) async-start(bf16[128,9,128]{2,1,0:T(8,128)(2,1)} %copy.100), calls=%async_computation.2 | async-start | bytes 1048576 | tf_op jit(solution)/shard_map/all_to_all | solution.py:26
  128.8 11.9 %copy-start.8 = (f32[8,1152]{1,0:T(8,128)S(1)}, f32[8,1152]{1,0:T(8,128)}, u32[]{:S(2)}) copy-start(f32[8,1152]{1,0:T(8,128)} %param.22) | copy-start | bytes 110596
  158.2 17.4 %all-to-all-start.3 = ((bf16[128,2,576]{2,1,0:T(2,128)(2,1)}), bf16[128,2,576]{2,1,0:T(2,128)(2,1)}, u32[]{:S(2)}, u32[]{:S(2)}) async-start(bf16[128,2,576]{2,1,0:T(2,128)(2,1)} %reshape.244), calls=%async_computation.3 | async-start | bytes 655360 | tf_op jit(solution)/shard_map/all_to_all | solution.py:22
  166.4 30.6 %collective-permute-start.3 = (bf16[1,8,256,128]{2,3,1,0:T(8,128)(2,1)}, bf16[1,8,256,128]{2,3,1,0:T(8,128)(2,1)}, u32[]{:S(2)}, u32[]{:S(2)}) collective-permute-start(bf16[1,8,256,128]{2,3,1,0:T(8,128)(2,1)} %bitcast.17), channel_id=1, source_target_pairs={{1,0},{2,1},{3,2},{4,3},{5,4},{6,5},{7,6},{8,7},{9,8},{10,9},{11,1... | collective-permute-start | bytes 1572872 | tf_op jit(solution)/shard_map/ppermute | solution.py:13
  173.7 23.4 %collective-permute-start.2 = (bf16[1,8,256,128]{2,3,1,0:T(8,128)(2,1)}, bf16[1,8,256,128]{2,3,1,0:T(8,128)(2,1)}, u32[]{:S(2)}, u32[]{:S(2)}) collective-permute-start(bf16[1,8,256,128]{2,3,1,0:T(8,128)(2,1)} %bitcast.17), channel_id=1, source_target_pairs={{0,1},{1,2},{2,3},{3,4},{4,5},{5,6},{6,7},{7,8},{8,9},{9,10},{10,1... | collective-permute-start | bytes 1572872 | tf_op jit(solution)/shard_map/ppermute | solution.py:13
  187.2 28.4 %all-to-all-start.4 = ((bf16[128,9,128]{2,1,0:T(8,128)(2,1)}), bf16[128,9,128]{2,1,0:T(8,128)(2,1)S(1)}, u32[]{:S(2)}, u32[]{:S(2)}) async-start(bf16[128,9,128]{2,1,0:T(8,128)(2,1)} %copy.108), calls=%async_computation.4 | async-start | bytes 1048576 | tf_op jit(solution)/shard_map/all_to_all | solution.py:26
  234.5 21.6 %all-to-all-start.5 = ((bf16[128,2,576]{2,1,0:T(2,128)(2,1)}), bf16[128,2,576]{2,1,0:T(2,128)(2,1)S(1)}, u32[]{:S(2)}, u32[]{:S(2)}) async-start(bf16[128,2,576]{2,1,0:T(2,128)(2,1)} %reshape.246), calls=%async_computation.5 | async-start | bytes 655360 | tf_op jit(solution)/shard_map/all_to_all | solution.py:22
  246.9 30.9 %collective-permute-start.5 = (bf16[1,8,256,128]{2,3,1,0:T(8,128)(2,1)}, bf16[1,8,256,128]{2,3,1,0:T(8,128)(2,1)}, u32[]{:S(2)}, u32[]{:S(2)}) collective-permute-start(bf16[1,8,256,128]{2,3,1,0:T(8,128)(2,1)} %bitcast.35), channel_id=1, source_target_pairs={{1,0},{2,1},{3,2},{4,3},{5,4},{6,5},{7,6},{8,7},{9,8},{10,9},{11,1... | collective-permute-start | bytes 1572872 | tf_op jit(solution)/shard_map/ppermute | solution.py:13
  253.8 24.0 %collective-permute-start.4 = (bf16[1,8,256,128]{2,3,1,0:T(8,128)(2,1)}, bf16[1,8,256,128]{2,3,1,0:T(8,128)(2,1)}, u32[]{:S(2)}, u32[]{:S(2)}) collective-permute-start(bf16[1,8,256,128]{2,3,1,0:T(8,128)(2,1)} %bitcast.35), channel_id=1, source_target_pairs={{0,1},{1,2},{2,3},{3,4},{4,5},{5,6},{6,7},{7,8},{8,9},{9,10},{10,1... | collective-permute-start | bytes 1572872 | tf_op jit(solution)/shard_map/ppermute | solution.py:13
  267.4 28.8 %all-to-all-start.6 = ((bf16[128,9,128]{2,1,0:T(8,128)(2,1)}), bf16[128,9,128]{2,1,0:T(8,128)(2,1)}, u32[]{:S(2)}, u32[]{:S(2)}) async-start(bf16[128,9,128]{2,1,0:T(8,128)(2,1)} %copy.115), calls=%async_computation.6 | async-start | bytes 1048576 | tf_op jit(solution)/shard_map/all_to_all | solution.py:26
  316.0 21.8 %all-to-all-start.7 = ((bf16[128,2,576]{2,1,0:T(2,128)(2,1)}), bf16[128,2,576]{2,1,0:T(2,128)(2,1)}, u32[]{:S(2)}, u32[]{:S(2)}) async-start(bf16[128,2,576]{2,1,0:T(2,128)(2,1)} %reshape.248), calls=%async_computation.7 | async-start | bytes 655360 | tf_op jit(solution)/shard_map/all_to_all | solution.py:22
  328.8 30.5 %collective-permute-start.7 = (bf16[1,8,256,128]{2,3,1,0:T(8,128)(2,1)}, bf16[1,8,256,128]{2,3,1,0:T(8,128)(2,1)}, u32[]{:S(2)}, u32[]{:S(2)}) collective-permute-start(bf16[1,8,256,128]{2,3,1,0:T(8,128)(2,1)} %bitcast.52), channel_id=1, source_target_pairs={{1,0},{2,1},{3,2},{4,3},{5,4},{6,5},{7,6},{8,7},{9,8},{10,9},{11,1... | collective-permute-start | bytes 1572872 | tf_op jit(solution)/shard_map/ppermute | solution.py:13
  335.7 23.6 %collective-permute-start.6 = (bf16[1,8,256,128]{2,3,1,0:T(8,128)(2,1)}, bf16[1,8,256,128]{2,3,1,0:T(8,128)(2,1)}, u32[]{:S(2)}, u32[]{:S(2)}) collective-permute-start(bf16[1,8,256,128]{2,3,1,0:T(8,128)(2,1)} %bitcast.52), channel_id=1, source_target_pairs={{0,1},{1,2},{2,3},{3,4},{4,5},{5,6},{6,7},{7,8},{8,9},{9,10},{10,1... | collective-permute-start | bytes 1572872 | tf_op jit(solution)/shard_map/ppermute | solution.py:13
  349.4 25.8 %all-to-all-start.8 = ((bf16[128,9,128]{2,1,0:T(8,128)(2,1)}), bf16[128,9,128]{2,1,0:T(8,128)(2,1)S(1)}, u32[]{:S(2)}, u32[]{:S(2)}) async-start(bf16[128,9,128]{2,1,0:T(8,128)(2,1)} %copy.122), calls=%async_computation.8 | async-start | bytes 1048576 | tf_op jit(solution)/shard_map/all_to_all | solution.py:26
  (2 other events, 15.8 us)
where the time goes:
time: 391 us; the launch traced here: 384 us
  local copies, waits for them, and re-layouts  133 us (34%)
  starting transfers between devices  121 us (31%)
  matrix products  76 us (19%)
  other arithmetic  45.6 us (12%)
  waiting for transfers between devices  7.73 us (2%)
    dot_general x4, matrix products, on_device(): jnp.einsum('gnlef,gnlfr->ger', near_blocks, picked * live_slots, preferre...  47.4 us
    all_to_all x5, starting transfers between devices, to_bands(): lax.all_to_all(spectra, ('grp', 'dir'), split_axis=1, concat_axis=0, tile...  43.6 us
    all_to_all x4, starting transfers between devices, from_bands(): lax.all_to_all(incoming, ('grp', 'dir'), split_axis=0, concat_axis=1, til...  39.3 us
    ppermute x8, starting transfers between devices, shifted(): return lax.ppermute(block, axis, route)  37.8 us
    unnamed x5, other arithmetic  36.1 us
    all_to_all x10, local copies, waits for them, and re-layouts, to_bands(): lax.all_to_all(spectra, ('grp', 'dir'), split_axis=1, concat_axis=0, tile...  34.6 us
    unnamed x36, local copies, waits for them, and re-layouts  30.4 us
    gather x5, local copies, waits for them, and re-layouts, on_device(): windows[lag_index][local_ids]  18.8 us
  transfers between devices with their start and end apart: 17, of which 2 were waited for; matrix products, arithmetic and copies ran while one was open for 40% of the time, Pallas kernels for 0%

commit v1 on v0

v1 whole, which is shorter than its diff:
```python
import functools

import jax
import jax.numpy as jnp
import numpy as np
from jax import lax
from jax.experimental import pallas as pl
from jax.experimental.pallas import tpu as pltpu
from jax.sharding import PartitionSpec as P

LAGS = 2
STEPS = 4
AXES = ("grp", "dir")
CHUNK = 16
BF16 = jnp.bfloat16
F32 = jnp.float32
MIB = 1 << 20


def params(mib, *semantics):
    return pltpu.CompilerParams(
        vmem_limit_bytes=mib * MIB, dimension_semantics=semantics or None
    )


def matmul(left, right):
    return jnp.dot(left, right, preferred_element_type=F32)


def spread_matrix(band, rows):
    out = np.zeros((CHUNK * rows, CHUNK * band), np.float32)
    for b in range(CHUNK):
        for i in range(band):
            out[b * rows + i, b * band + i] = 1.0
    return out


def lagged_spread(band, rows):
    out = np.zeros((LAGS, CHUNK * LAGS * rows, CHUNK * band), np.float32)
    for lag in range(LAGS):
        for b in range(CHUNK):
            for i in range(band):
                out[lag, (b * LAGS + lag) * rows + i, b * band + i] = 1.0
    return out


def pack_kernel(select_ref, past_ref, out_ref):
    tall, wide = select_ref.shape[1], select_ref.shape[2]
    for m in range(past_ref.shape[1] // wide):
        total = matmul(select_ref[0], past_ref[0, pl.ds(m * wide, wide), :])
        for lag in range(1, LAGS):
            total += matmul(select_ref[lag], past_ref[lag, pl.ds(m * wide, wide), :])
        out_ref[pl.ds(m * tall, tall), :] = total.astype(BF16)


def pack(past, band, rows):
    select = jnp.asarray(lagged_spread(band, rows), BF16)
    messages = past.shape[1] // band
    return pl.pallas_call(
        pack_kernel,
        out_shape=jax.ShapeDtypeStruct((messages * LAGS * rows, past.shape[2]), BF16),
        compiler_params=params(16),
        name="pack",
    )(select, past)


def rays_kernel(select_ref, ray_in_ref, ray_out_ref, shift_ref, in_ref, out_ref, shift_out_ref):
    tall, wide = select_ref.shape
    select = select_ref[...]
    outgoing = ray_out_ref[...].astype(F32).T
    shift = shift_ref[...]
    shift = jnp.concatenate([shift, jnp.zeros((128 - shift.shape[0], shift.shape[1]), F32)]).T
    incoming = []
    for m in range(ray_in_ref.shape[0] // wide):
        at, to = m * wide, pl.ds(m * tall, tall)
        incoming.append(matmul(select, ray_in_ref[pl.ds(at, wide), :]))
        out_ref[to, :] = matmul(select, outgoing[at : at + wide, :].astype(BF16)).astype(BF16)
        rest = shift[at : at + wide, :]
        total = jnp.zeros((tall, 128), F32)
        for _ in range(3):
            piece = rest.astype(BF16)
            total += matmul(select, piece)
            rest = rest - piece.astype(F32)
        shift_out_ref[to, :] = total
    in_ref[...] = jnp.concatenate(incoming).T.astype(BF16)


def pad_rays(ray_in, ray_out, child_shift, band, rows):
    select = jnp.asarray(spread_matrix(band, rows), BF16)
    padded = ray_in.shape[0] // band * rows
    return pl.pallas_call(
        rays_kernel,
        out_shape=(
            jax.ShapeDtypeStruct((ray_in.shape[1], padded), BF16),
            jax.ShapeDtypeStruct((padded, ray_out.shape[0]), BF16),
            jax.ShapeDtypeStruct((padded, 128), F32),
        ),
        compiler_params=params(32),
        name="rays",
    )(select, ray_in, ray_out, child_shift)


def weights_kernel(rows, repeat_ref, block_ref, residue_ref, lanes_ref, slots_ref, table_ref, out_ref, wide_ref, keep_ref):
    @pl.when(pl.program_id(0) == 0)
    def _():
        slot = lax.broadcasted_iota(jnp.int32, wide_ref.shape, 0)
        column = lax.broadcasted_iota(jnp.int32, wide_ref.shape, 1)
        offset = column - slot * rows
        inside = jnp.logical_and(offset >= 0, offset < rows)
        wide_ref[...] = jnp.where(inside, 1.0, 0.0).astype(BF16)
        same = residue_ref[...] == lanes_ref[...]
        keep_ref[...] = jnp.where(same, 1.0, 0.0).astype(BF16)

    table = table_ref[...].T.astype(BF16)
    spread = (matmul(repeat_ref[...], table) * block_ref[...]).astype(BF16)
    columns = lax.broadcasted_iota(jnp.int32, (slots_ref.shape[0], wide_ref.shape[0]), 1)
    onehot = jnp.where(slots_ref[...] == columns, 1.0, 0.0).astype(BF16)
    merged = matmul(spread, onehot).astype(BF16)
    out_ref[...] = matmul(merged, wide_ref[...]).astype(BF16) * keep_ref[...]


def far_weights(far_sources, far_delays, translation, rows):
    parents, entries, band = translation.shape
    slots = LAGS * parents
    tall, deep = CHUNK * rows, CHUNK * entries
    slot_index = ((far_delays - 1) * parents + far_sources).reshape(parents * entries, 1)
    table = jnp.pad(translation.reshape(parents * entries, band), ((0, 0), (0, 128 - band)))
    repeat = np.zeros((tall, 128), np.float32)
    repeat[np.arange(tall), np.arange(tall) % rows] = 1.0
    block = (np.arange(tall)[:, None] // rows == np.arange(deep)[None, :] // entries).astype(np.float32)
    residue = (np.arange(tall) % rows).astype(np.int32)[:, None]
    lanes = (np.arange(slots * rows) % rows).astype(np.int32)[None, :]
    whole = lambda i: (0, 0)
    return pl.pallas_call(
        functools.partial(weights_kernel, rows),
        grid=(parents // CHUNK,),
        in_specs=[
            pl.BlockSpec(repeat.shape, whole),
            pl.BlockSpec(block.shape, whole),
            pl.BlockSpec(residue.shape, whole),
            pl.BlockSpec(lanes.shape, whole),
            pl.BlockSpec((deep, 1), lambda i: (i, 0)),
            pl.BlockSpec((deep, 128), lambda i: (i, 0)),
        ],
        out_specs=pl.BlockSpec((tall, slots * rows), lambda i: (i, 0)),
        out_shape=jax.ShapeDtypeStruct((parents * rows, slots * rows), BF16),
        scratch_shapes=[
            pltpu.VMEM((slots, slots * rows), BF16),
            pltpu.VMEM((tall, slots * rows), BF16),
        ],
        compiler_params=params(32, "arbitrary"),
        name="weights",
    )(jnp.asarray(repeat, BF16), jnp.asarray(block), jnp.asarray(residue), jnp.asarray(lanes), slot_index, table)


def translate_kernel(weights_ref, newest_ref, oldest_ref, out_ref):
    depth = newest_ref.shape[0]
    total = matmul(weights_ref[:, :depth], newest_ref[...])
    total += matmul(weights_ref[:, depth:], oldest_ref[...])
    out_ref[...] = total.astype(BF16)


def translate(weights, newest, oldest):
    tall, columns = newest.shape
    tile = 256
    return pl.pallas_call(
        translate_kernel,
        grid=(tall // tile,),
        in_specs=[
            pl.BlockSpec((tile, weights.shape[1]), lambda i: (i, 0)),
            pl.BlockSpec((tall, columns), lambda i: (0, 0)),
            pl.BlockSpec((tall, columns), lambda i: (0, 0)),
        ],
        out_specs=pl.BlockSpec((tile, columns), lambda i: (i, 0)),
        out_shape=jax.ShapeDtypeStruct((tall, columns), BF16),
        compiler_params=params(16, "arbitrary"),
        name="translate",
    )(weights, newest, oldest)


def near_kernel(leads, ids_ref, mask_ref, incident_ref, blocks_ref, *refs):
    sources, (out_ref, window_ref, sems) = refs[: 3 * LAGS], refs[3 * LAGS :]
    groups = out_ref.shape[0] if len(out_ref.shape) == 4 else window_ref.shape[1] // 3
    slots = blocks_ref.shape[1]
    g = pl.program_id(0)

    @pl.when(g == 0)
    def _():
        copies = []
        for lag in range(LAGS):
            for side in range(3):
                source = sources[lag * 3 + side]
                if leads[lag] is not None:
                    source = source.at[leads[lag]]
                copies.append(
                    pltpu.make_async_copy(
                        source, window_ref.at[lag, pl.ds(side * groups, groups)], sems.at[lag * 3 + side]
                    )
                )
        for copy in copies:
            copy.start()
        for copy in copies:
            copy.wait()

    total = incident_ref[0, 0]
    for n in range(slots):
        local = ids_ref[g * slots + n]
        live = mask_ref[g * slots + n] != 0
        for lag in range(LAGS):
            picked = window_ref[lag, local]
            picked = jnp.where(live, picked, jnp.zeros_like(picked))
            total -= matmul(blocks_ref[0, n, lag], picked)
    out_ref[0] = total


def near_field(local_ids, live_slots, incident, step, near_blocks, windows):
    groups, slots, lags, unknowns, _ = near_blocks.shape
    columns = incident.shape[3]
    arrays = [array for parts, _ in windows for array in parts]
    leads = tuple(lead for _, lead in windows)
    return pl.pallas_call(
        functools.partial(near_kernel, leads),
        grid_spec=pltpu.PrefetchScalarGridSpec(
            num_scalar_prefetch=2,
            grid=(groups,),
            in_specs=[
                pl.BlockSpec((1, 1, unknowns, columns), lambda g, ids, mask: (step, g, 0, 0)),
                pl.BlockSpec((1, slots, lags, unknowns, unknowns), lambda g, ids, mask: (g, 0, 0, 0, 0)),
            ]
            + [pl.BlockSpec(memory_space=pl.ANY)] * len(arrays),
            out_specs=pl.BlockSpec((1, unknowns, columns), lambda g, ids, mask: (g, 0, 0)),
            scratch_shapes=[
                pltpu.VMEM((lags, 3 * groups, unknowns, columns), BF16),
                pltpu.SemaphoreType.DMA((3 * lags,)),
            ],
        ),
        out_shape=jax.ShapeDtypeStruct((groups, unknowns, columns), F32),
        compiler_params=params(16, "arbitrary"),
        name="near",
    )(local_ids, live_slots, incident, near_blocks, *arrays)


def solve_kernel(last, aliased, *refs):
    arriving_ref, base_ref, inverse_ref, in_ref, outward_ref, shift_ref = refs[:6]
    outs = refs[7:] if aliased else refs[6:]
    results_ref = outs[0]
    children, unknowns, columns = base_ref.shape
    arriving = arriving_ref[...].astype(F32)
    spectra = None
    for c in range(0, children, 2):
        pair = (c, c + 1)
        received = jnp.concatenate(
            [(shift_ref[:, d : d + 1] * arriving).astype(BF16) for d in pair], axis=1
        )
        fields = matmul(in_ref[...], received)
        currents = []
        for i, d in enumerate(pair):
            drive = (base_ref[d] - fields[:, i * columns : (i + 1) * columns]).astype(BF16)
            current = matmul(inverse_ref[d], drive).astype(BF16)
            results_ref[0, d] = current
            if not last:
                outs[1][d] = current
            currents.append(current)
        if not last:
            spread = matmul(outward_ref[...], jnp.concatenate(currents, axis=1))
            for i, d in enumerate(pair):
                term = shift_ref[:, d : d + 1] * spread[:, i * columns : (i + 1) * columns]
                spectra = term if spectra is None else spectra + term
    if not last:
        outs[2][...] = spectra.astype(BF16)


def solve(step, results, arriving, base, self_inverse, ray_in, ray_out, shift):
    last = step == STEPS - 1
    groups, unknowns, columns = base.shape
    operands = [arriving, base, self_inverse, ray_in, ray_out, shift]
    in_specs = [pl.BlockSpec(a.shape, functools.partial(lambda n, i: (0,) * n, a.ndim)) for a in operands]
    aliases = {}
    if results is not None:
        aliases = {len(operands): 0}
        operands.append(results)
        in_specs.append(pl.BlockSpec(memory_space=pl.ANY))
    out_shape = [jax.ShapeDtypeStruct((STEPS, groups, unknowns, columns), BF16)]
    out_specs = [pl.BlockSpec((1, groups, unknowns, columns), lambda i: (step, 0, 0, 0))]
    if not last:
        out_shape += [
            jax.ShapeDtypeStruct((groups, unknowns, columns), BF16),
            jax.ShapeDtypeStruct(arriving.shape, BF16),
        ]
        out_specs += [
            pl.BlockSpec((groups, unknowns, columns), lambda i: (0, 0, 0)),
            pl.BlockSpec(arriving.shape, lambda i: (0, 0)),
        ]
    return pl.pallas_call(
        functools.partial(solve_kernel, last, results is not None),
        grid=(1,),
        in_specs=in_specs,
        out_specs=out_specs,
        out_shape=out_shape,
        input_output_aliases=aliases,
        compiler_params=params(32, "arbitrary"),
        name="solve",
    )(*operands)


def shifted(block, distance):
    devices = range(lax.axis_size(AXES))
    route = [(i - distance, i) for i in devices if i - distance in devices]
    return lax.ppermute(block, AXES, route)


def window(block):
    return [shifted(block, 1), block, shifted(block, -1)]


def exchange(block, messages):
    tall, columns = block.shape
    cut = block.reshape(messages, tall // messages // 2, 2, columns)
    moved = lax.all_to_all(cut, AXES, split_axis=0, concat_axis=0, tiled=True)
    return moved.reshape(tall, columns)


def exchange_past(past, band, rows):
    packed = pack(past, band, rows)
    columns = packed.shape[1]
    messages = packed.shape[0] // (LAGS * rows)
    cut = packed.reshape(messages, LAGS * rows // 2, 2, columns)
    moved = lax.all_to_all(cut, AXES, split_axis=0, concat_axis=0, tiled=True)
    moved = moved.reshape(messages, LAGS, rows // 2, 2, columns)
    return [moved[:, lag].reshape(messages * rows, columns) for lag in range(LAGS)]


def on_device(
    incident,
    currents_past,
    spectra_past,
    self_inverse,
    near_blocks,
    neighbours,
    near_mask,
    ray_out,
    ray_in,
    child_shift,
    far_sources,
    far_delays,
    translation,
):
    groups = self_inverse.shape[0]
    messages, band = translation.shape[0], translation.shape[2]
    rows = band + band % 2
    first_group = (lax.axis_index(AXES) - 1) * groups
    local_ids = (neighbours - first_group).reshape(-1)
    live_slots = near_mask.reshape(-1)
    bands = exchange_past(spectra_past[:, 0], band, rows)
    past = window(currents_past)
    windows = [(past, 0), (past, 1)]
    rays = pad_rays(ray_in, ray_out, child_shift, band, rows)
    weights = far_weights(far_sources, far_delays, translation, rows)
    results = None
    for step in range(STEPS):
        arriving = exchange(translate(weights, bands[0], bands[1]), messages)
        base = near_field(local_ids, live_slots, incident, step, near_blocks, windows)
        results, *rest = solve(step, results, arriving, base, self_inverse, *rays)
        if rest:
            current, spectra = rest
            windows = [(window(current), None), windows[0]]
            bands = [exchange(spectra, messages), bands[0]]
    return results


def solution(mesh):
    in_specs = (
        P(None, AXES, None, None),
        P(None, AXES, None, None),
        P(None, AXES, None, None),
        P(AXES, None, None),
        P(AXES, None, None, None, None),
        P(AXES, None),
        P(AXES, None),
        P(),
        P(),
        P(),
        P(),
        P(),
        P(None, None, AXES),
    )
    out_specs = P(None, AXES, None, None)
    return jax.shard_map(
        on_device, mesh=mesh, in_specs=in_specs, out_specs=out_specs, check_vma=False
    )
```

time: 391 us -> 262 us (0.67); the launches traced: 384 us -> 260 us
  matrix products: 76 us -> 0 us
  Pallas kernels: 0 us -> 68.6 us
  local copies, waits for them, and re-layouts: 133 us -> 71.7 us
  other arithmetic: 45.6 us -> 0.01 us
  starting transfers between devices: 121 us -> 111 us
    dot_general x16 -> x0, matrix products: 76 us -> none  [the longest x4 47.4 us: on_device(): jnp.einsum('gnlef,gnlfr->ger', near_blocks, picked * live_slots, preferre...]
    pallas_call x0 -> x15, Pallas kernels: none -> 68.6 us  [the longest x4 27.6 us: near_field(): pl.pallas_call(functools.partial(near_kernel, leads), grid_spec=pltpu.Pre...]
    unnamed x36 -> x103, local copies, waits for them, and re-layouts: 30.4 us -> 67.7 us
    unnamed x5 -> x0, other arithmetic: 36.1 us -> none
    all_to_all x10 -> x1, local copies, waits for them, and re-layouts: 34.6 us -> 1.21 us  [exchange_past(): moved = lax.all_to_all(cut, AXES, split_axis=0, concat_axis=0, tiled=True)]
    gather x5 -> x0, local copies, waits for them, and re-layouts: 18.8 us -> none  [on_device(): windows[lag_index][local_ids]]
    convert_element_type x15 -> x0, local copies, waits for them, and re-layouts: 17 us -> none  [the longest x8 7.78 us: on_device(): child_shift[None, :, :, None] * arriving[:, None]]
    squeeze x4 -> x0, local copies, waits for them, and re-layouts: 12.3 us -> none  [the longest x3 10.3 us: on_device(): bands = [to_bands(spectra_past[lag_index]) for lag_index in range(LAGS)]]
  transfers between devices with their start and end apart: 17 -> 16, of which waited for: 2 -> 6; matrix products, arithmetic and copies ran while one was open for 40% -> 2% of each run, Pallas kernels for 0% -> 19%
where the time goes in v1:
time: 262 us; the launch traced here: 260 us
  starting transfers between devices  111 us (42%)
  local copies, waits for them, and re-layouts  71.7 us (27%)
  Pallas kernels  68.6 us (26%)
  waiting for transfers between devices  7.28 us (3%)
    unnamed x103, local copies, waits for them, and re-layouts  67.7 us
    all_to_all x7, starting transfers between devices, exchange(): moved = lax.all_to_all(cut, AXES, split_axis=0, concat_axis=0, tiled=True)  63.5 us
    ppermute x8, starting transfers between devices, shifted(): return lax.ppermute(block, AXES, route)  36 us
    pallas_call x4, Pallas kernels, near_field(): pl.pallas_call(functools.partial(near_kernel, leads), grid_spec=pltpu.Pre...  27.6 us
    pallas_call x4, Pallas kernels, solve(): pl.pallas_call(functools.partial(solve_kernel, last, results is not None)...  17.9 us
    pallas_call x4, Pallas kernels, translate(): pl.pallas_call(translate_kernel, grid=(tall // tile,), in_specs=[pl.Block...  13.7 us
    all_to_all x1, starting transfers between devices, exchange_past(): moved = lax.all_to_all(cut, AXES, split_axis=0, concat_axis=0, tiled=True)  11.9 us
    pallas_call x1, Pallas kernels, far_weights(): pl.pallas_call(functools.partial(weights_kernel, rows), grid=(parents //...  6.6 us
  transfers between devices with their start and end apart: 16, of which 6 were waited for; matrix products, arithmetic and copies ran while one was open for 2% of the time, Pallas kernels for 19%

profile of v1, /device:TPU:1, one launch (start us, length us, event | category | flops | bytes accessed | tf_op | source)
XLA Modules:
  0.0 259.5 jit_solution(10084430310601081262)
XLA Ops:
  3.7 11.9 %all-to-all-start = ((bf16[128,10,2,128]{3,2,1,0:T(2,128)(2,1)}), bf16[128,10,2,128]{3,2,1,0:T(2,128)(2,1)}, u32[]{:S(2)}, u32[]{:S(2)}) async-start(bf16[128,10,2,128]{3,2,1,0:T(2,128)(2,1)} %bitcast.2), calls=%async_computation | async-start | bytes 1310720 | tf_op jit(solution)/shard_map/all_to_all | solution.py:328
  15.6 7.0 %collective-permute-start.1 = (bf16[2,8,256,128]{3,2,1,0:T(8,128)(2,1)}, bf16[2,8,256,128]{3,2,1,0:T(8,128)(2,1)}, u32[]{:S(2)}, u32[]{:S(2)}) collective-permute-start(bf16[2,8,256,128]{3,2,1,0:T(8,128)(2,1)} %refs_4_.3), channel_id=1, source_target_pairs={{1,0},{2,1},{3,2},{4,3},{5,4},{6,5},{7,6},{8,7},{9,8},{10,9},{11,1... | collective-permute-start | bytes 3145736 | tf_op jit(solution)/shard_map/ppermute | solution.py:309
  28.0 6.6 %weights.1.weights_ref = bf16[1280,2560]{1,0:T(8,128)(2,1)S(1)} custom-call(bf16[160,128]{1,0:T(8,128)(2,1)S(1)} %copy-done.43, f32[160,256]{1,0:T(8,128)S(1)} %copy-done.40, s32[160,1]{1,0:T(8,128)S(1)} %copy-done.41, s32[1,2560]{1,0:T(1,128)S(1)} %copy-done.45, s32[2048,1]{1,0:T(8,128)S(1)} %reshape.80.slots_ref, f32[2048,128]{1,0:T(8,128)S(1)} %pad.4.table_ref), custom_call_target="tpu_custom_call" | custom-call | tf_op jit(solution)/shard_map/weights/pallas_call | solution.py:134
  45.5 10.3 %all-to-all-start.1 = ((bf16[128,5,2,128]{3,2,1,0:T(2,128)(2,1)}), bf16[128,5,2,128]{3,2,1,0:T(2,128)(2,1)}, u32[]{:S(2)}, u32[]{:S(2)}) async-start(bf16[128,5,2,128]{3,2,1,0:T(2,128)(2,1)} %bitcast.6), calls=%async_computation.1 | async-start | bytes 655360 | tf_op jit(solution)/shard_map/all_to_all | solution.py:319
  59.3 4.6 %copy-done = bf16[8,6,2,256,256]{4,3,2,1,0:T(8,128)(2,1)S(1)} copy-done((bf16[8,6,2,256,256]{4,3,2,1,0:T(8,128)(2,1)S(1)}, bf16[8,6,2,256,256]{4,3,2,1,0:T(8,128)(2,1)}, u32[]{:S(2)}) %copy-start) | copy-done | bytes 12582936
  66.0 7.1 %near.4.refs_1_ = f32[8,256,128]{2,1,0:T(8,128)S(1)} custom-call(s32[48]{0:T(128)S(1)} %reshape.66.ids_ref, s32[48]{0:T(128)S(1)} %reshape.67.mask_ref, f32[4,8,256,128]{3,2,1,0:T(8,128)S(1)} %copy-done.9, bf16[8,6,2,256,256]{4,3,2,1,0:T(8,128)(2,1)S(1)} %copy-done, bf16[2,8,256,128]{3,2,1,0:T(8,128)(2,1)} %collective-permute-done.refs_0_.refs_3_, ...), custom_call_target="tpu_custom_call" | custom-call | tf_op jit(solution)/shard_map/near/pallas_call | solution.py:221
  75.4 5.0 %solve.4 = (bf16[4,8,256,128]{3,2,1,0:T(8,128)(2,1)}, bf16[8,256,128]{2,1,0:T(8,128)(2,1)S(1)}, bf16[1280,128]{1,0:T(8,128)(2,1)S(1)}) custom-call(bf16[1280,128]{1,0:T(8,128)(2,1)} %bitcast.7.refs_0_, f32[8,256,128]{2,1,0:T(8,128)S(1)} %copy-done.17, bf16[8,256,256]{2,1,0:T(8,128)(2,1)S(1)} %copy-done.13, bf16[256,1280]{1,0:T(8,128)(2,1)S(1)} %get-tuple-element.17.refs_3_, ...), custom_call_target="tpu_custom_call" | custom-call | tf_op jit(solution)/shard_map/solve/pallas_call | solution.py:294
  81.9 10.2 %all-to-all-start.2 = ((bf16[128,5,2,128]{3,2,1,0:T(2,128)(2,1)}), bf16[128,5,2,128]{3,2,1,0:T(2,128)(2,1)}, u32[]{:S(2)}, u32[]{:S(2)}) async-start(bf16[128,5,2,128]{3,2,1,0:T(2,128)(2,1)} %bitcast.33), calls=%async_computation.2 | async-start | bytes 655360 | tf_op jit(solution)/shard_map/all_to_all | solution.py:319
  92.1 7.0 %collective-permute-start.3 = (bf16[8,256,128]{2,1,0:T(8,128)(2,1)}, bf16[8,256,128]{2,1,0:T(8,128)(2,1)}, u32[]{:S(2)}, u32[]{:S(2)}) collective-permute-start(bf16[8,256,128]{2,1,0:T(8,128)(2,1)} %copy-done.22), channel_id=1, source_target_pairs={{1,0},{2,1},{3,2},{4,3},{5,4},{6,5},{7,6},{8,7},{9,8},{10,9},{11,1... | collective-permute-start | bytes 1572872 | tf_op jit(solution)/shard_map/ppermute | solution.py:309
  110.3 7.9 %all-to-all-start.3 = ((bf16[128,5,2,128]{3,2,1,0:T(2,128)(2,1)}), bf16[128,5,2,128]{3,2,1,0:T(2,128)(2,1)S(1)}, u32[]{:S(2)}, u32[]{:S(2)}) async-start(bf16[128,5,2,128]{3,2,1,0:T(2,128)(2,1)} %bitcast.28), calls=%async_computation.3 | async-start | bytes 655360 | tf_op jit(solution)/shard_map/all_to_all | solution.py:319
  118.5 4.6 %copy-done.1 = bf16[8,6,2,256,256]{4,3,2,1,0:T(8,128)(2,1)S(1)} copy-done((bf16[8,6,2,256,256]{4,3,2,1,0:T(8,128)(2,1)S(1)}, bf16[8,6,2,256,256]{4,3,2,1,0:T(8,128)(2,1)}, u32[]{:S(2)}) %copy-start.1) | copy-done | bytes 12582936
  126.3 6.9 %near.5.refs_1_ = f32[8,256,128]{2,1,0:T(8,128)S(1)} custom-call(s32[48]{0:T(128)S(1)} %reshape.66.ids_ref, s32[48]{0:T(128)S(1)} %reshape.67.mask_ref, f32[4,8,256,128]{3,2,1,0:T(8,128)S(1)} %copy-done.10, bf16[8,6,2,256,256]{4,3,2,1,0:T(8,128)(2,1)S(1)} %copy-done.1, bf16[8,256,128]{2,1,0:T(8,128)(2,1)} %collective-permute-done.2.refs_0_.refs_3_, ...), custom_call_target="tpu_custom_call" | custom-call | tf_op jit(solution)/shard_map/near/pallas_call | solution.py:221
  135.5 4.3 %solve.5 = (bf16[4,8,256,128]{3,2,1,0:T(8,128)(2,1)}, bf16[8,256,128]{2,1,0:T(8,128)(2,1)S(1)}, bf16[1280,128]{1,0:T(8,128)(2,1)S(1)}) custom-call(bf16[1280,128]{1,0:T(8,128)(2,1)S(1)} %bitcast.25, f32[8,256,128]{2,1,0:T(8,128)S(1)} %copy-done.15, bf16[8,256,256]{2,1,0:T(8,128)(2,1)S(1)} %copy-done.13, ...), custom_call_target="tpu_custom_call", output_to_operand_aliasing={{0}: (6, {})} | custom-call | tf_op jit(solution)/shard_map/solve/pallas_call | solution.py:294
  141.4 9.5 %all-to-all-start.4 = ((bf16[128,5,2,128]{3,2,1,0:T(2,128)(2,1)}), bf16[128,5,2,128]{3,2,1,0:T(2,128)(2,1)S(1)}, u32[]{:S(2)}, u32[]{:S(2)}) async-start(bf16[128,5,2,128]{3,2,1,0:T(2,128)(2,1)} %bitcast.31), calls=%async_computation.4 | async-start | bytes 655360 | tf_op jit(solution)/shard_map/all_to_all | solution.py:319
  150.9 7.0 %collective-permute-start.5 = (bf16[8,256,128]{2,1,0:T(8,128)(2,1)}, bf16[8,256,128]{2,1,0:T(8,128)(2,1)}, u32[]{:S(2)}, u32[]{:S(2)}) collective-permute-start(bf16[8,256,128]{2,1,0:T(8,128)(2,1)} %copy-done.25), channel_id=1, source_target_pairs={{1,0},{2,1},{3,2},{4,3},{5,4},{6,5},{7,6},{8,7},{9,8},{10,9},{11,1... | collective-permute-start | bytes 1572872 | tf_op jit(solution)/shard_map/ppermute | solution.py:309
  169.4 7.8 %all-to-all-start.5 = ((bf16[128,5,2,128]{3,2,1,0:T(2,128)(2,1)}), bf16[128,5,2,128]{3,2,1,0:T(2,128)(2,1)}, u32[]{:S(2)}, u32[]{:S(2)}) async-start(bf16[128,5,2,128]{3,2,1,0:T(2,128)(2,1)} %bitcast.27), calls=%async_computation.5 | async-start | bytes 655360 | tf_op jit(solution)/shard_map/all_to_all | solution.py:319
  177.3 4.6 %copy-done.2 = bf16[8,6,2,256,256]{4,3,2,1,0:T(8,128)(2,1)S(1)} copy-done((bf16[8,6,2,256,256]{4,3,2,1,0:T(8,128)(2,1)S(1)}, bf16[8,6,2,256,256]{4,3,2,1,0:T(8,128)(2,1)}, u32[]{:S(2)}) %copy-start.2) | copy-done | bytes 12582936
  186.1 6.8 %near.6.refs_1_ = f32[8,256,128]{2,1,0:T(8,128)S(1)} custom-call(s32[48]{0:T(128)S(1)} %reshape.66.ids_ref, s32[48]{0:T(128)S(1)} %reshape.67.mask_ref, f32[4,8,256,128]{3,2,1,0:T(8,128)S(1)} %copy-done.11, bf16[8,6,2,256,256]{4,3,2,1,0:T(8,128)(2,1)S(1)} %copy-done.2, bf16[8,256,128]{2,1,0:T(8,128)(2,1)} %collective-permute-done.4.refs_0_.refs_3_, ...), custom_call_target="tpu_custom_call" | custom-call | tf_op jit(solution)/shard_map/near/pallas_call | solution.py:221
  195.1 5.3 %solve.6 = (bf16[4,8,256,128]{3,2,1,0:T(8,128)(2,1)}, bf16[8,256,128]{2,1,0:T(8,128)(2,1)S(1)}, bf16[1280,128]{1,0:T(8,128)(2,1)S(1)}) custom-call(bf16[1280,128]{1,0:T(8,128)(2,1)} %bitcast.15.refs_0_, f32[8,256,128]{2,1,0:T(8,128)S(1)} %copy-done.19, bf16[8,256,256]{2,1,0:T(8,128)(2,1)S(1)} %copy-done.13, ...), custom_call_target="tpu_custom_call", output_to_operand_aliasing={{0}: (6, {})} | custom-call | tf_op jit(solution)/shard_map/solve/pallas_call | solution.py:294
  201.9 10.1 %all-to-all-start.6 = ((bf16[128,5,2,128]{3,2,1,0:T(2,128)(2,1)}), bf16[128,5,2,128]{3,2,1,0:T(2,128)(2,1)}, u32[]{:S(2)}, u32[]{:S(2)}) async-start(bf16[128,5,2,128]{3,2,1,0:T(2,128)(2,1)} %bitcast.32), calls=%async_computation.6 | async-start | bytes 655360 | tf_op jit(solution)/shard_map/all_to_all | solution.py:319
  212.0 7.0 %collective-permute-start.7 = (bf16[8,256,128]{2,1,0:T(8,128)(2,1)}, bf16[8,256,128]{2,1,0:T(8,128)(2,1)}, u32[]{:S(2)}, u32[]{:S(2)}) collective-permute-start(bf16[8,256,128]{2,1,0:T(8,128)(2,1)} %copy-done.34), channel_id=1, source_target_pairs={{1,0},{2,1},{3,2},{4,3},{5,4},{6,5},{7,6},{8,7},{9,8},{10,9},{11,1... | collective-permute-start | bytes 1572872 | tf_op jit(solution)/shard_map/ppermute | solution.py:309
  230.2 7.9 %all-to-all-start.7 = ((bf16[128,5,2,128]{3,2,1,0:T(2,128)(2,1)}), bf16[128,5,2,128]{3,2,1,0:T(2,128)(2,1)S(1)}, u32[]{:S(2)}, u32[]{:S(2)}) async-start(bf16[128,5,2,128]{3,2,1,0:T(2,128)(2,1)} %bitcast.26), calls=%async_computation.7 | async-start | bytes 655360 | tf_op jit(solution)/shard_map/all_to_all | solution.py:319
  238.4 4.6 %copy-done.3 = bf16[8,6,2,256,256]{4,3,2,1,0:T(8,128)(2,1)S(1)} copy-done((bf16[8,6,2,256,256]{4,3,2,1,0:T(8,128)(2,1)S(1)}, bf16[8,6,2,256,256]{4,3,2,1,0:T(8,128)(2,1)}, u32[]{:S(2)}) %copy-start.3) | copy-done | bytes 12582936
  247.2 6.8 %near.7.refs_1_ = f32[8,256,128]{2,1,0:T(8,128)S(1)} custom-call(s32[48]{0:T(128)S(1)} %reshape.66.ids_ref, s32[48]{0:T(128)S(1)} %reshape.67.mask_ref, f32[4,8,256,128]{3,2,1,0:T(8,128)S(1)} %copy-done.12, bf16[8,6,2,256,256]{4,3,2,1,0:T(8,128)(2,1)S(1)} %copy-done.3, bf16[8,256,128]{2,1,0:T(8,128)(2,1)} %collective-permute-done.6.refs_0_, ...), custom_call_target="tpu_custom_call" | custom-call | tf_op jit(solution)/shard_map/near/pallas_call | solution.py:221
  (137 shorter events, 88.6 us)
Async XLA Ops:
  2.0 22.5 %copy-start.47 = (s32[128,16]{0,1:T(8,128)S(1)}, s32[128,16]{0,1:T(8,128)}, u32[]{:S(2)}) copy-start(s32[128,16]{0,1:T(8,128)} %param.29) | copy-start | bytes 24580
  2.0 22.5 %copy-start.48 = (s32[128,16]{0,1:T(8,128)S(1)}, s32[128,16]{0,1:T(8,128)}, u32[]{:S(2)}) copy-start(s32[128,16]{0,1:T(8,128)} %param.30) | copy-start | bytes 24580
  2.0 23.2 %copy-start.46 = (f32[128,16,9]{0,1,2:T(8,128)S(1)}, f32[128,16,9]{0,1,2:T(8,128)}, u32[]{:S(2)}) copy-start(f32[128,16,9]{0,1,2:T(8,128)} %param.31) | copy-start | bytes 221188
  3.7 33.6 %all-to-all-start = ((bf16[128,10,2,128]{3,2,1,0:T(2,128)(2,1)}), bf16[128,10,2,128]{3,2,1,0:T(2,128)(2,1)}, u32[]{:S(2)}, u32[]{:S(2)}) async-start(bf16[128,10,2,128]{3,2,1,0:T(2,128)(2,1)} %bitcast.2), calls=%async_computation | async-start | bytes 1310720 | tf_op jit(solution)/shard_map/all_to_all | solution.py:328
  15.6 43.6 %collective-permute-start.1 = (bf16[2,8,256,128]{3,2,1,0:T(8,128)(2,1)}, bf16[2,8,256,128]{3,2,1,0:T(8,128)(2,1)}, u32[]{:S(2)}, u32[]{:S(2)}) collective-permute-start(bf16[2,8,256,128]{3,2,1,0:T(8,128)(2,1)} %refs_4_.3), channel_id=1, source_target_pairs={{1,0},{2,1},{3,2},{4,3},{5,4},{6,5},{7,6},{8,7},{9,8},{10,9},{11,1... | collective-permute-start | bytes 3145736 | tf_op jit(solution)/shard_map/ppermute | solution.py:309
  22.6 36.7 %collective-permute-start = (bf16[2,8,256,128]{3,2,1,0:T(8,128)(2,1)}, bf16[2,8,256,128]{3,2,1,0:T(8,128)(2,1)}, u32[]{:S(2)}, u32[]{:S(2)}) collective-permute-start(bf16[2,8,256,128]{3,2,1,0:T(8,128)(2,1)} %refs_4_.3), channel_id=1, source_target_pairs={{0,1},{1,2},{2,3},{3,4},{4,5},{5,6},{6,7},{7,8},{8,9},{9,10},{10,1... | collective-permute-start | bytes 3145736 | tf_op jit(solution)/shard_map/ppermute | solution.py:309
  42.2 13.7 %copy-start.49 = (s32[8,6]{1,0:T(8,128)S(1)}, s32[8,6]{1,0:T(8,128)}, u32[]{:S(2)}) copy-start(s32[8,6]{1,0:T(8,128)} %param.25) | copy-start | bytes 580
  42.2 13.7 %copy-start.50 = (s32[8,6]{1,0:T(8,128)S(1)}, s32[8,6]{1,0:T(8,128)}, u32[]{:S(2)}) copy-start(s32[8,6]{1,0:T(8,128)} %param.24) | copy-start | bytes 580
  42.2 13.8 %copy-start.42 = (bf16[160,144]{1,0:T(8,128)(2,1)S(1)}, bf16[160,144]{1,0:T(8,128)(2,1)}, u32[]{:S(2)}) copy-start(bf16[160,144]{1,0:T(8,128)(2,1)} %constant.36.clone.select_ref) | copy-start | bytes 138244
  42.2 13.8 %copy-start.44 = (f32[8,1152]{1,0:T(8,128)S(1)}, f32[8,1152]{1,0:T(8,128)}, u32[]{:S(2)}) copy-start(f32[8,1152]{1,0:T(8,128)} %shift_ref.1) | copy-start | bytes 110596
  45.5 28.6 %all-to-all-start.1 = ((bf16[128,5,2,128]{3,2,1,0:T(2,128)(2,1)}), bf16[128,5,2,128]{3,2,1,0:T(2,128)(2,1)}, u32[]{:S(2)}, u32[]{:S(2)}) async-start(bf16[128,5,2,128]{3,2,1,0:T(2,128)(2,1)} %bitcast.6), calls=%async_computation.1 | async-start | bytes 655360 | tf_op jit(solution)/shard_map/all_to_all | solution.py:319
  58.1 16.0 %copy-start.13 = (bf16[8,256,256]{2,1,0:T(8,128)(2,1)S(1)}, bf16[8,256,256]{2,1,0:T(8,128)(2,1)}, u32[]{:S(2)}) copy-start(bf16[8,256,256]{2,1,0:T(8,128)(2,1)} %refs_2_.7) | copy-start | bytes 3145732
  81.9 21.3 %all-to-all-start.2 = ((bf16[128,5,2,128]{3,2,1,0:T(2,128)(2,1)}), bf16[128,5,2,128]{3,2,1,0:T(2,128)(2,1)}, u32[]{:S(2)}, u32[]{:S(2)}) async-start(bf16[128,5,2,128]{3,2,1,0:T(2,128)(2,1)} %bitcast.33), calls=%async_computation.2 | async-start | bytes 655360 | tf_op jit(solution)/shard_map/all_to_all | solution.py:319
  92.1 26.1 %collective-permute-start.3 = (bf16[8,256,128]{2,1,0:T(8,128)(2,1)}, bf16[8,256,128]{2,1,0:T(8,128)(2,1)}, u32[]{:S(2)}, u32[]{:S(2)}) collective-permute-start(bf16[8,256,128]{2,1,0:T(8,128)(2,1)} %copy-done.22), channel_id=1, source_target_pairs={{1,0},{2,1},{3,2},{4,3},{5,4},{6,5},{7,6},{8,7},{9,8},{10,9},{11,1... | collective-permute-start | bytes 1572872 | tf_op jit(solution)/shard_map/ppermute | solution.py:309
  99.1 19.4 %collective-permute-start.2 = (bf16[8,256,128]{2,1,0:T(8,128)(2,1)}, bf16[8,256,128]{2,1,0:T(8,128)(2,1)}, u32[]{:S(2)}, u32[]{:S(2)}) collective-permute-start(bf16[8,256,128]{2,1,0:T(8,128)(2,1)} %copy-done.22), channel_id=1, source_target_pairs={{0,1},{1,2},{2,3},{3,4},{4,5},{5,6},{6,7},{7,8},{8,9},{9,10},{10,1... | collective-permute-start | bytes 1572872 | tf_op jit(solution)/shard_map/ppermute | solution.py:309
  110.3 24.0 %all-to-all-start.3 = ((bf16[128,5,2,128]{3,2,1,0:T(2,128)(2,1)}), bf16[128,5,2,128]{3,2,1,0:T(2,128)(2,1)S(1)}, u32[]{:S(2)}, u32[]{:S(2)}) async-start(bf16[128,5,2,128]{3,2,1,0:T(2,128)(2,1)} %bitcast.28), calls=%async_computation.3 | async-start | bytes 655360 | tf_op jit(solution)/shard_map/all_to_all | solution.py:319
  141.4 20.9 %all-to-all-start.4 = ((bf16[128,5,2,128]{3,2,1,0:T(2,128)(2,1)}), bf16[128,5,2,128]{3,2,1,0:T(2,128)(2,1)S(1)}, u32[]{:S(2)}, u32[]{:S(2)}) async-start(bf16[128,5,2,128]{3,2,1,0:T(2,128)(2,1)} %bitcast.31), calls=%async_computation.4 | async-start | bytes 655360 | tf_op jit(solution)/shard_map/all_to_all | solution.py:319
  150.9 26.3 %collective-permute-start.5 = (bf16[8,256,128]{2,1,0:T(8,128)(2,1)}, bf16[8,256,128]{2,1,0:T(8,128)(2,1)}, u32[]{:S(2)}, u32[]{:S(2)}) collective-permute-start(bf16[8,256,128]{2,1,0:T(8,128)(2,1)} %copy-done.25), channel_id=1, source_target_pairs={{1,0},{2,1},{3,2},{4,3},{5,4},{6,5},{7,6},{8,7},{9,8},{10,9},{11,1... | collective-permute-start | bytes 1572872 | tf_op jit(solution)/shard_map/ppermute | solution.py:309
  157.8 19.4 %collective-permute-start.4 = (bf16[8,256,128]{2,1,0:T(8,128)(2,1)}, bf16[8,256,128]{2,1,0:T(8,128)(2,1)}, u32[]{:S(2)}, u32[]{:S(2)}) collective-permute-start(bf16[8,256,128]{2,1,0:T(8,128)(2,1)} %copy-done.25), channel_id=1, source_target_pairs={{0,1},{1,2},{2,3},{3,4},{4,5},{5,6},{6,7},{7,8},{8,9},{9,10},{10,1... | collective-permute-start | bytes 1572872 | tf_op jit(solution)/shard_map/ppermute | solution.py:309
  169.4 24.5 %all-to-all-start.5 = ((bf16[128,5,2,128]{3,2,1,0:T(2,128)(2,1)}), bf16[128,5,2,128]{3,2,1,0:T(2,128)(2,1)}, u32[]{:S(2)}, u32[]{:S(2)}) async-start(bf16[128,5,2,128]{3,2,1,0:T(2,128)(2,1)} %bitcast.27), calls=%async_computation.5 | async-start | bytes 655360 | tf_op jit(solution)/shard_map/all_to_all | solution.py:319
  201.9 21.2 %all-to-all-start.6 = ((bf16[128,5,2,128]{3,2,1,0:T(2,128)(2,1)}), bf16[128,5,2,128]{3,2,1,0:T(2,128)(2,1)}, u32[]{:S(2)}, u32[]{:S(2)}) async-start(bf16[128,5,2,128]{3,2,1,0:T(2,128)(2,1)} %bitcast.32), calls=%async_computation.6 | async-start | bytes 655360 | tf_op jit(solution)/shard_map/all_to_all | solution.py:319
  212.0 26.1 %collective-permute-start.7 = (bf16[8,256,128]{2,1,0:T(8,128)(2,1)}, bf16[8,256,128]{2,1,0:T(8,128)(2,1)}, u32[]{:S(2)}, u32[]{:S(2)}) collective-permute-start(bf16[8,256,128]{2,1,0:T(8,128)(2,1)} %copy-done.34), channel_id=1, source_target_pairs={{1,0},{2,1},{3,2},{4,3},{5,4},{6,5},{7,6},{8,7},{9,8},{10,9},{11,1... | collective-permute-start | bytes 1572872 | tf_op jit(solution)/shard_map/ppermute | solution.py:309
  219.0 19.4 %collective-permute-start.6 = (bf16[8,256,128]{2,1,0:T(8,128)(2,1)}, bf16[8,256,128]{2,1,0:T(8,128)(2,1)}, u32[]{:S(2)}, u32[]{:S(2)}) collective-permute-start(bf16[8,256,128]{2,1,0:T(8,128)(2,1)} %copy-done.34), channel_id=1, source_target_pairs={{0,1},{1,2},{2,3},{3,4},{4,5},{5,6},{6,7},{7,8},{8,9},{9,10},{10,1... | collective-permute-start | bytes 1572872 | tf_op jit(solution)/shard_map/ppermute | solution.py:309
  230.2 24.8 %all-to-all-start.7 = ((bf16[128,5,2,128]{3,2,1,0:T(2,128)(2,1)}), bf16[128,5,2,128]{3,2,1,0:T(2,128)(2,1)S(1)}, u32[]{:S(2)}, u32[]{:S(2)}) async-start(bf16[128,5,2,128]{3,2,1,0:T(2,128)(2,1)} %bitcast.26), calls=%async_computation.7 | async-start | bytes 655360 | tf_op jit(solution)/shard_map/all_to_all | solution.py:319
  (43 other events, 79.7 us)
